TPU v7x, 32 devices: a whole 2x2x4 slice. The times are simulated.
32 devices in a mesh: rows: 16 (over z, x, core), freq: 2 (over y).
Axes of the slice: x: 2, y: 2, z: 4, core: 2. Of those that a mesh axis runs over, the one named last changes fastest.
Arguments:
- design: float32 [128, 65536], P('rows'), may hold values from 0.05 to 0.95
- passive: int32 [128, 65536], P('rows'), may hold values 0 or 1
- state: bfloat16 [2, 2, 128, 65536], P(None, 'freq', 'rows'), may hold values from -36 to 36
- adjoint: bfloat16 [2, 2, 128, 65536], P(None, 'freq', 'rows'), may hold values from -36 to 36
- omega_sq: float32 [2], replicated, may hold values from 0.05 to 2
- assign: int32 [2], P('freq'), may hold values from 0 to 1, each once
Outputs:
- gradient: float32 [128, 65536], P('rows')
Inputs may be any that keep to these rules, and one draw needn't show every extreme that they name: `assign`: each of 0 .. 1 appears once.
All inputs are finite; a program needn't handle non-finite values. No bound on the sum of `passive` on one device may be relied on, other than what follows from the above.
Results may differ from a plain program's by a relative error of at most 0.0003.
Values may be sent and summed in bfloat16 or wider, within the bound.
A program may use at most 128 MiB of HBM per device.

v0:
```python
import jax
import jax.numpy as jnp
from jax import lax
from jax.sharding import PartitionSpec as P

RADIUS = 8
sharpness = 8.0
threshold = 0.5
exponent = 3.0
soft_floor = 0.001
loss_factor = 0.2
epsilon = 1e-06
stiff_table = [
    [4.0 / 6, -1.0 / 6, -1.0 / 6, -2.0 / 6],
    [-1.0 / 6, 4.0 / 6, -2.0 / 6, -1.0 / 6],
    [-1.0 / 6, -2.0 / 6, 4.0 / 6, -1.0 / 6],
    [-2.0 / 6, -1.0 / 6, -1.0 / 6, 4.0 / 6],
]
mass_table = [
    [4.0 / 36, 2.0 / 36, 2.0 / 36, 1.0 / 36],
    [2.0 / 36, 4.0 / 36, 1.0 / 36, 2.0 / 36],
    [2.0 / 36, 1.0 / 36, 4.0 / 36, 2.0 / 36],
    [1.0 / 36, 2.0 / 36, 2.0 / 36, 4.0 / 36],
]


def extended(block, sides, width):
    for axis, dim in sides:
        count = lax.axis_size(axis)
        forward = [(i, i + 1) for i in range(count - 1)]
        backward = [(target, source) for source, target in forward]
        low = lax.ppermute(
            lax.slice_in_dim(block, block.shape[dim] - width, None, axis=dim), axis, forward
        )
        high = lax.ppermute(lax.slice_in_dim(block, 0, width, axis=dim), axis, backward)
        block = jnp.concatenate([low, block, high], axis=dim)
    return block


def from_behind(block, axis, distance):
    devices = range(lax.axis_size(axis))
    route = [(i - distance, i) for i in devices if i - distance in devices]
    return lax.ppermute(block, axis, route)


def tap_list():
    return [float(RADIUS + 1 - abs(offset)) for offset in range(-RADIUS, RADIUS + 1)]


def row_pass(padded, count):
    taps = tap_list()
    total = taps[0] * padded[0:count]
    for offset in range(1, 2 * RADIUS + 1):
        total = total + taps[offset] * padded[offset : offset + count]
    return total


def col_pass(field):
    taps = tap_list()
    count = field.shape[1]
    padded = jnp.pad(field, ((0, 0), (RADIUS, RADIUS)))
    total = taps[0] * padded[:, 0:count]
    for offset in range(1, 2 * RADIUS + 1):
        total = total + taps[offset] * padded[:, offset : offset + count]
    return total


def edge_sums(start, count, whole):
    positions = start + jnp.arange(count, dtype=jnp.int32)
    total = jnp.zeros((count,), jnp.float32)
    for offset in range(-RADIUS, RADIUS + 1):
        inside = ((positions + offset >= 0) & (positions + offset < whole)).astype(jnp.float32)
        total = total + float(RADIUS + 1 - abs(offset)) * inside
    return total


def project(tilde, passive):
    bottom = jnp.tanh(sharpness * threshold) + jnp.tanh(sharpness * (1.0 - threshold))
    steep = jnp.tanh(sharpness * (tilde - threshold))
    value = (jnp.tanh(sharpness * threshold) + steep) / bottom
    slope = sharpness * (1.0 - steep * steep) / bottom
    solid = passive > 0
    density = jnp.where(solid, 1.0, value)
    slope = jnp.where(solid, 0.0, slope)
    stiffness = exponent * density * density * (1.0 - soft_floor)
    return (stiffness, slope)


def bilinear(table, left, right):
    total = None
    for row_pos in range(4):
        inner = table[row_pos][0] * right[0]
        for col_pos in range(1, 4):
            inner = inner + table[row_pos][col_pos] * right[col_pos]
        term = left[row_pos] * inner
        total = term if total is None else total + term
    return total


def corners(nodes, below):
    stacked = jnp.concatenate([nodes, below], axis=0)
    right_col = jnp.zeros((stacked.shape[0], 1), stacked.dtype)
    shifted = jnp.concatenate([stacked[:, 1:], right_col], axis=1)
    return (stacked[:-1], shifted[:-1], stacked[1:], shifted[1:])


def element_terms(fields, fields_below, duals, duals_below, stiffness, omega):
    state_real = corners(fields[0], fields_below[0])
    state_imag = corners(fields[1], fields_below[1])
    adjoint_real = corners(duals[0], duals_below[0])
    adjoint_imag = corners(duals[1], duals_below[1])
    elastic = bilinear(stiff_table, adjoint_real, state_real) - bilinear(
        stiff_table, adjoint_imag, state_imag
    )
    damped = bilinear(stiff_table, adjoint_real, state_imag) + bilinear(
        stiff_table, adjoint_imag, state_real
    )
    inertia = bilinear(mass_table, adjoint_real, state_real) - bilinear(
        mass_table, adjoint_imag, state_imag
    )
    return stiffness * (elastic - loss_factor * damped) - omega * inertia


def shards(design, passive, state, adjoint, omega_sq, assign):
    slab_rows, width = design.shape
    whole_rows = slab_rows * lax.axis_size("rows")
    top = lax.axis_index("rows") * slab_rows
    weight_sum = (
        edge_sums(top, slab_rows, whole_rows)[:, None] * edge_sums(0, width, width)[None, :]
    )
    padded = extended(design, (("rows", 0),), RADIUS)
    tilde = col_pass(row_pass(padded, slab_rows)) / weight_sum
    stiffness, slope = project(tilde, passive)
    factor = slope / weight_sum
    below_state, below_adjoint = from_behind((state[:, :, :1, :], adjoint[:, :, :1, :]), "rows", -1)
    table = jnp.arange(omega_sq.shape[0], dtype=jnp.int32)
    picked = (assign[:, None] == table[None, :]).astype(jnp.float32)
    omegas = jnp.sum(picked * omega_sq[None, :], axis=1)

    def accumulate(slot, total):
        fields = lax.dynamic_index_in_dim(state, slot, 1, keepdims=False).astype(jnp.float32)
        duals = lax.dynamic_index_in_dim(adjoint, slot, 1, keepdims=False).astype(jnp.float32)
        fields_below = lax.dynamic_index_in_dim(below_state, slot, 1, keepdims=False).astype(
            jnp.float32
        )
        duals_below = lax.dynamic_index_in_dim(below_adjoint, slot, 1, keepdims=False).astype(
            jnp.float32
        )
        omega = lax.dynamic_index_in_dim(omegas, slot, 0, keepdims=False)
        return total + element_terms(fields, fields_below, duals, duals_below, stiffness, omega)

    local = lax.fori_loop(0, state.shape[1], accumulate, jnp.zeros((slab_rows, width), jnp.float32))
    share = lax.psum_scatter(local, "freq", scatter_dimension=1, tiled=True)
    piece_cols = share.shape[1]
    start = lax.axis_index("freq") * piece_cols
    spread = share * lax.dynamic_slice_in_dim(factor, start, piece_cols, 1)
    padded_back = extended(spread, (("rows", 0),), RADIUS)
    rowed = row_pass(padded_back, slab_rows)
    joined = lax.all_gather(rowed, "freq", axis=1, tiled=True)
    back = col_pass(joined)
    total = lax.psum(jnp.sum(back * back), "rows")
    return back * lax.rsqrt(total / (whole_rows * width) + epsilon)


def solution(mesh):
    return jax.shard_map(
        shards,
        mesh=mesh,
        in_specs=(
            P("rows", None),
            P("rows", None),
            P(None, "freq", "rows", None),
            P(None, "freq", "rows", None),
            P(),
            P("freq"),
        ),
        out_specs=P("rows", None),
        check_vma=False,
    )
```

profile of v0, /device:TPU:0, one launch (start us, length us, event | category | flops | bytes accessed | tf_op | source)
XLA Modules:
  0.0 300.1 jit_solution(13670841534242166203)
XLA Ops:
  6.5 0.0 copy-start.4
  6.5 0.0 reduce-scatter.2.cloned.1.call-start
  6.5 3.9 %collective-permute-start = (f32[8,65536]{1,0:T(8,128)}, f32[8,65536]{1,0:T(8,128)}, u32[]{:S(2)}, u32[]{:S(2)}) collective-permute-start(f32[8,65536]{1,0:T(8,128)} %param.6), channel_id=1, source_target_pairs={{0,2},{2,4},{4,6},{6,8},{8,10},{10,12},{12,14},{14,16},{16,18},{18... | collective-permute-start | bytes 6291464 | tf_op jit(solution)/shard_map/ppermute | solution.py:32
  10.4 1.3 collective-permute-start.1
  11.7 1.9 slice.352
  13.6 0.4 copy.9
  14.0 1.3 collective-permute-start.2
  15.3 1.9 slice.358
  17.2 1.1 copy.10
  18.3 0.0 copy-start.5
  18.3 1.4 collective-permute-start.3
  19.7 0.0 copy-done.4
  19.7 0.3 convert_element_type.103
  20.0 0.0 copy-done.5
  20.0 0.3 convert_element_type.102
  20.3 1.6 slice_bitcast_fusion.2
  21.9 0.0 copy-start.9
  21.9 2.2 slice_bitcast_fusion.3
  24.8 0.0 copy-start.1
  24.8 0.0 copy-done.9
  24.8 0.6 fusion.172
  25.4 0.0 collective-permute-done.2
  25.4 0.2 convert_element_type.104
  25.6 0.4 slice_bitcast_fusion.7
  26.0 0.0 collective-permute-done.3
  26.0 1.1 convert_element_type.105
  27.1 0.4 slice_bitcast_fusion.6
  27.6 0.0 copy-start.6
  27.6 0.0 copy-start.7
  27.6 0.0 copy-done.1
  27.6 0.0 copy-start
  27.6 6.6 %slice_maximum_fusion = (f32[9,65535]{1,0:T(8,128)}, f32[9,65535]{1,0:T(8,128)}) fusion(f32[1,65536]{1,0:T(1,128)S(1)} %get-tuple-element.46, f32[8,65536]{1,0:T(8,128)} %get-tuple-element.36, f32[1,65536]{1,0:T(1,128)S(1)} %get-tuple-element.45, f32[8,65536]{1,0:T(8,128)S(1)} %copy-done.1), kind=kLoop, calls=%fused_computation | loop fusion | flops 1179630 | bytes 9437112 | tf_op jit(solution)/shard_map/while/body/eval_jaxpr/concatenate | solution.py:101
  34.2 0.0 copy-done.6
  34.2 0.0 copy-done.7
  34.2 0.0 copy-done
  34.2 4.9 %slice_maximum_fusion.1 = (f32[9,65535]{1,0:T(8,128)}, f32[9,65535]{1,0:T(8,128)}) fusion(f32[1,65536]{1,0:T(1,128)S(1)} %get-tuple-element.44, f32[8,65536]{1,0:T(8,128)S(1)} %copy-done, f32[1,65536]{1,0:T(1,128)S(1)} %get-tuple-element.43, f32[8,65536]{1,0:T(8,128)S(1)} %get-tuple-element.38), kind=kLoop, calls=%fused_computation.1 | loop fusion | flops 1179630 | bytes 9437112 | tf_op jit(solution)/shard_map/while/body/eval_jaxpr/concatenate | solution.py:101
  39.1 0.0 copy-start.2
  39.1 0.0 collective-permute-done
  39.1 1.9 constant_dynamic-update-slice_fusion.1
  41.0 0.3 copy-done.2
  41.3 0.3 constant_dynamic-update-slice_fusion
  41.6 0.0 collective-permute-done.1
  41.6 1.7 constant_dynamic-update-slice_fusion.2
  43.3 6.9 %fusion.4 = f32[8,65536]{1,0:T(8,128)} fusion(f32[8,65536]{1,0:T(8,128)} %collective-permute-done.1, f32[16,65536]{1,0:T(8,128)S(1)} %constant_dynamic-update-slice_fusion.2, f32[16,65536]{1,0:T(8,128)S(1)} %get-tuple-element.41, f32[8,65536]{1,0:T(8,128)} %collective-permute-done, f32[8,65536]{1,0:T(8,128)} %param.6), kind=kLoop, calls=%fused_computation.67 | loop fusion | flops 16252928 | bytes 37748736 | tf_op jit(solution)/shard_map/add | solution.py:54
  50.2 46.0 %fusion.2 = (f32[8,65536]{1,0:T(8,128)}, f32[8,65536]{1,0:T(8,128)}, pred[8,65536]{1,0:T(8,128)(4,1)}) fusion(f32[8,65536]{1,0:T(8,128)} %get-tuple-element.40, f32[8,65536]{1,0:T(8,128)} %get-tuple-element.36, f32[8,65536]{1,0:T(8,128)S(1)} %get-tuple-element.38, f32[8,65536]{1,0:T(8,128)} %get-tuple-element.26, f32[1,65536]{1,0:T(1,128)} %copy-done.7, ...), kind=kLoop, calls=%fused_computation.56 | loop fusion | flops 100663296 | bytes 28049300 | tf_op jit(solution)/shard_map/while/body/eval_jaxpr/sub | solution.py:121
  96.2 0.0 copy-start.3
  96.2 0.0 copy-start.8
  96.2 0.0 reduce-scatter.2.cloned.1.call-update
  96.2 0.0 all-gather.2.cloned.1.call-start
  96.3 1.5 broadcast_multiply_fusion.1
  97.8 69.1 %reduce-scatter.2.cloned.1.call-done = f32[8,32768]{1,0:T(8,128)} async-done(((f32[8,65536]{1,0:T(8,128)}), f32[8,32768]{1,0:T(8,128)}) %reduce-scatter.2.cloned.1.call-update) | async-done | bytes 1048592 | tf_op jit(solution)/shard_map/reduce_scatter | solution.py:153
  166.9 0.0 copy-done.3
  166.9 0.0 copy-done.8
  166.9 1.9 fusion.104
  168.7 1.3 collective-permute-start.5
  170.0 3.1 %collective-permute-start.4 = (f32[8,32768]{1,0:T(8,128)S(1)}, f32[8,32768]{1,0:T(8,128)S(1)}, u32[]{:S(2)}, u32[]{:S(2)}) collective-permute-start(f32[8,32768]{1,0:T(8,128)S(1)} %fusion.104), channel_id=1, source_target_pairs={{0,2},{2,4},{4,6},{6,8},{8,10},{10,12},{12,14},{14,16},{16,18},{18... | collective-permute-start | bytes 3145736 | tf_op jit(solution)/shard_map/ppermute | solution.py:32
  173.1 0.1 collective-permute-done.5
  173.3 2.1 collective-permute-done.4
  175.3 4.2 %fusion.66 = f32[8,32768]{1,0:T(8,128)} fusion(f32[8,32768]{1,0:T(8,128)S(1)} %collective-permute-done.5, f32[8,32768]{1,0:T(8,128)S(1)} %fusion.104, f32[8,32768]{1,0:T(8,128)S(1)} %collective-permute-done.4), kind=kLoop, calls=%fused_computation.159 | loop fusion | flops 11796480 | bytes 4194304 | tf_op jit(solution)/shard_map/add | solution.py:54
  179.6 0.0 all-gather.2.cloned.1.call-update
  179.6 53.8 %all-gather.2.cloned.1.call-done = f32[8,65536]{1,0:T(8,128)} async-done(((f32[8,32768]{1,0:T(8,128)}), f32[8,65536]{1,0:T(8,128)}) %all-gather.2.cloned.1.call-update) | async-done | bytes 2097168 | tf_op jit(solution)/shard_map/all_gather | solution.py:159
  233.4 24.1 %multiply_reduce_fusion = (f32[]{:T(128)}, f32[8,65536]{1,0:T(8,128)S(1)}) fusion(f32[8,65536]{1,0:T(8,128)} %all-gather.2.cloned.1.call-done), kind=kLoop, calls=%fused_computation.95 | loop fusion | flops 17301504 | bytes 4194308 | tf_op jit(solution)/shard_map/reduce_sum | solution.py:161
  257.5 33.6 %psum.7 = f32[]{:T(128)} all-reduce(f32[]{:T(128)} %get-tuple-element.21), channel_id=1, replica_groups=mesh['rows'=16,'freq'=2] {'rows'}, use_global_device_ids=true, to_apply=%region_3.4 | all-reduce | flops 1 | bytes 8 | tf_op jit(solution)/shard_map/psum | solution.py:161
  291.8 1.5 broadcast_multiply_fusion
  (2 shorter events, 0.0 us)
Async XLA Ops:
  6.5 13.2 %copy-start.4 = (bf16[2,1,8,65536]{3,2,1,0:T(8,128)(2,1)S(1)}, bf16[2,1,8,65536]{3,2,1,0:T(8,128)(2,1)}, u32[]{:S(2)}) copy-start(bf16[2,1,8,65536]{3,2,1,0:T(8,128)(2,1)} %param.8) | copy-start | bytes 6291460
  6.5 160.3 %reduce-scatter.2.cloned.1.call-start = ((), (), s32[]{:S(2)}) async-start(), calls=%async_computation.1 | async-start | bytes 3145728 | tf_op jit(solution)/shard_map/reduce_scatter | solution.py:153
  6.5 32.5 %collective-permute-start = (f32[8,65536]{1,0:T(8,128)}, f32[8,65536]{1,0:T(8,128)}, u32[]{:S(2)}, u32[]{:S(2)}) collective-permute-start(f32[8,65536]{1,0:T(8,128)} %param.6), channel_id=1, source_target_pairs={{0,2},{2,4},{4,6},{6,8},{8,10},{10,12},{12,14},{14,16},{16,18},{18... | collective-permute-start | bytes 6291464 | tf_op jit(solution)/shard_map/ppermute | solution.py:32
  10.4 31.2 %collective-permute-start.1 = (f32[8,65536]{1,0:T(8,128)}, f32[8,65536]{1,0:T(8,128)}, u32[]{:S(2)}, u32[]{:S(2)}) collective-permute-start(f32[8,65536]{1,0:T(8,128)} %param.6), channel_id=1, source_target_pairs={{2,0},{4,2},{6,4},{8,6},{10,8},{12,10},{14,12},{16,14},{18,16},{20... | collective-permute-start | bytes 6291464 | tf_op jit(solution)/shard_map/ppermute | solution.py:35
  14.0 11.4 %collective-permute-start.2 = (bf16[2,1,1,65536]{3,0,2,1:T(2,128)(2,1)S(1)}, bf16[2,1,1,65536]{3,0,2,1:T(2,128)(2,1)S(1)}, u32[]{:S(2)}, u32[]{:S(2)}) collective-permute-start(bf16[2,1,1,65536]{3,0,2,1:T(2,128)(2,1)S(1)} %copy.9), channel_id=1, source_target_pairs={{2,0},{4,2},{6,4},{8,6},{10,8},{12,10},{14,12},{16,14},{18,16},{20... | collective-permute-start | bytes 786440 | tf_op jit(solution)/shard_map/ppermute | solution.py:43
  18.3 1.7 copy-start.5
  18.3 7.7 %collective-permute-start.3 = (bf16[2,1,1,65536]{3,0,2,1:T(2,128)(2,1)}, bf16[2,1,1,65536]{3,0,2,1:T(2,128)(2,1)}, u32[]{:S(2)}, u32[]{:S(2)}) collective-permute-start(bf16[2,1,1,65536]{3,0,2,1:T(2,128)(2,1)} %copy.10), channel_id=1, source_target_pairs={{2,0},{4,2},{6,4},{8,6},{10,8},{12,10},{14,12},{16,14},{18,16},{20... | collective-permute-start | bytes 786440 | tf_op jit(solution)/shard_map/ppermute | solution.py:43
  21.9 2.9 copy-start.9
  24.8 2.8 copy-start.1
  27.6 6.7 %copy-start.6 = (f32[1,65536]{1,0:T(1,128)}, f32[1,65536]{1,0:T(1,128)S(1)}, u32[]{:S(2)}) copy-start(f32[1,65536]{1,0:T(1,128)S(1)} %get-tuple-element.45) | copy-start | bytes 786436
  27.6 6.7 %copy-start.7 = (f32[1,65536]{1,0:T(1,128)}, f32[1,65536]{1,0:T(1,128)S(1)}, u32[]{:S(2)}) copy-start(f32[1,65536]{1,0:T(1,128)S(1)} %get-tuple-element.46) | copy-start | bytes 786436
  27.6 6.6 %copy-start = (f32[8,65536]{1,0:T(8,128)S(1)}, f32[8,65536]{1,0:T(8,128)}, u32[]{:S(2)}) copy-start(f32[8,65536]{1,0:T(8,128)} %get-tuple-element.40) | copy-start | bytes 6291460
  39.1 2.2 copy-start.2
  96.2 70.7 %copy-start.3 = (f32[8,65536]{1,0:T(8,128)S(1)}, f32[8,65536]{1,0:T(8,128)}, u32[]{:S(2)}) copy-start(f32[8,65536]{1,0:T(8,128)} %get-tuple-element.24) | copy-start | bytes 6291460
  96.2 70.7 %copy-start.8 = (pred[8,65536]{1,0:T(8,128)(4,1)S(1)}, pred[8,65536]{1,0:T(8,128)(4,1)}, u32[]{:S(2)}) copy-start(pred[8,65536]{1,0:T(8,128)(4,1)} %get-tuple-element.25) | copy-start | bytes 1572868
  96.2 137.2 %all-gather.2.cloned.1.call-start = ((), (), s32[]{:S(2)}) async-start(), calls=%async_computation.2 | async-start | bytes 3145728 | tf_op jit(solution)/shard_map/all_gather | solution.py:159
  168.7 4.6 %collective-permute-start.5 = (f32[8,32768]{1,0:T(8,128)S(1)}, f32[8,32768]{1,0:T(8,128)S(1)}, u32[]{:S(2)}, u32[]{:S(2)}) collective-permute-start(f32[8,32768]{1,0:T(8,128)S(1)} %fusion.104), channel_id=1, source_target_pairs={{2,0},{4,2},{6,4},{8,6},{10,8},{12,10},{14,12},{16,14},{18,16},{20... | collective-permute-start | bytes 3145736 | tf_op jit(solution)/shard_map/ppermute | solution.py:35
  170.0 5.3 %collective-permute-start.4 = (f32[8,32768]{1,0:T(8,128)S(1)}, f32[8,32768]{1,0:T(8,128)S(1)}, u32[]{:S(2)}, u32[]{:S(2)}) collective-permute-start(f32[8,32768]{1,0:T(8,128)S(1)} %fusion.104), channel_id=1, source_target_pairs={{0,2},{2,4},{4,6},{6,8},{8,10},{10,12},{12,14},{14,16},{16,18},{18... | collective-permute-start | bytes 3145736 | tf_op jit(solution)/shard_map/ppermute | solution.py:32
Sparse Core Ops, SparseCore 0:
  96.3 70.4 reduce-scatter.1
  179.7 53.6 all-gather.1
where the time goes:
time: 301 us; the launch traced here: 300 us
  waiting for transfers between devices  125 us (42%)
  other arithmetic  100 us (33%)
  blocking collectives  33.6 us (11%)
  between operations  15 us (5%)
  local copies, waits for them, and re-layouts  14.1 us (5%)
  starting transfers between devices  12.3 us (4%)
    reduce_scatter x1, waiting for transfers between devices, shards(): share = lax.psum_scatter(local, 'freq', scatter_dimension=1, tiled=True)  69.1 us
    all_gather x1, waiting for transfers between devices, shards(): joined = lax.all_gather(rowed, 'freq', axis=1, tiled=True)  53.8 us
    sub x1, other arithmetic, element_terms(): return stiffness * (elastic - loss_factor * damped) - omega * inertia  46 us
    psum x1, blocking collectives, shards(): total = lax.psum(jnp.sum(back * back), 'rows')  33.6 us
    reduce_sum x1, other arithmetic, shards(): total = lax.psum(jnp.sum(back * back), 'rows')  24.1 us
    concatenate x2, other arithmetic, corners(): stacked = jnp.concatenate([nodes, below], axis=0)  11.5 us
    add x2, other arithmetic, row_pass(): total = total + taps[offset] * padded[offset:offset + count]  11.1 us
    ppermute x2, starting transfers between devices, extended(): lax.ppermute(lax.slice_in_dim(block, block.shape[dim] - width, None, axis...  6.98 us
  transfers between devices with their start and end apart: 8, of which 4 were waited for; matrix products, arithmetic and copies ran while one was open for 9% of the time, Pallas kernels for 0%

commit v1 on v0

--- a/solution.py
+++ b/solution.py
@@ -156,7 +156,8 @@
     spread = share * lax.dynamic_slice_in_dim(factor, start, piece_cols, 1)
     padded_back = extended(spread, (("rows", 0),), RADIUS)
     rowed = row_pass(padded_back, slab_rows)
-    joined = lax.all_gather(rowed, "freq", axis=1, tiled=True)
+    parts = lax.all_gather(rowed, "freq", axis=0, tiled=False)
+    joined = jnp.concatenate(parts, axis=1)
     back = col_pass(joined)
     total = lax.psum(jnp.sum(back * back), "rows")
     return back * lax.rsqrt(total / (whole_rows * width) + epsilon)

time: 301 us -> 301 us (level)
  no operation moved by 1% of the time
where the time goes in v1:
time: 301 us; the launch traced here: 300 us
  waiting for transfers between devices  125 us (42%)
  other arithmetic  100 us (33%)
  blocking collectives  33.6 us (11%)
  between operations  15 us (5%)
  local copies, waits for them, and re-layouts  14.1 us (5%)
  starting transfers between devices  12.3 us (4%)
    reduce_scatter x1, waiting for transfers between devices, shards(): share = lax.psum_scatter(local, 'freq', scatter_dimension=1, tiled=True)  69.1 us
    all_gather x1, waiting for transfers between devices, shards(): parts = lax.all_gather(rowed, 'freq', axis=0, tiled=False)  53.8 us
    sub x1, other arithmetic, element_terms(): return stiffness * (elastic - loss_factor * damped) - omega * inertia  46 us
    psum x1, blocking collectives, shards(): total = lax.psum(jnp.sum(back * back), 'rows')  33.6 us
    reduce_sum x1, other arithmetic, shards(): total = lax.psum(jnp.sum(back * back), 'rows')  24.1 us
    concatenate x2, other arithmetic, corners(): stacked = jnp.concatenate([nodes, below], axis=0)  11.5 us
    add x2, other arithmetic, row_pass(): total = total + taps[offset] * padded[offset:offset + count]  11.1 us
    ppermute x2, starting transfers between devices, extended(): lax.ppermute(lax.slice_in_dim(block, block.shape[dim] - width, None, axis...  6.98 us
  transfers between devices with their start and end apart: 8, of which 4 were waited for; matrix products, arithmetic and copies ran while one was open for 9% of the time, Pallas kernels for 0%

profile of v1, /device:TPU:0, one launch (start us, length us, event | category | flops | bytes accessed | tf_op | source)
XLA Modules:
  0.0 300.1 jit_solution(13670841534242166203)
XLA Ops:
  6.5 0.0 copy-start.4
  6.5 0.0 reduce-scatter.2.cloned.1.call-start
  6.5 3.9 %collective-permute-start = (f32[8,65536]{1,0:T(8,128)}, f32[8,65536]{1,0:T(8,128)}, u32[]{:S(2)}, u32[]{:S(2)}) collective-permute-start(f32[8,65536]{1,0:T(8,128)} %param.6), channel_id=1, source_target_pairs={{0,2},{2,4},{4,6},{6,8},{8,10},{10,12},{12,14},{14,16},{16,18},{18... | collective-permute-start | bytes 6291464 | tf_op jit(solution)/shard_map/ppermute | solution.py:32
  10.4 1.3 collective-permute-start.1
  11.7 1.9 slice.352
  13.6 0.4 copy.9
  14.0 1.3 collective-permute-start.2
  15.3 1.9 slice.358
  17.2 1.1 copy.10
  18.3 0.0 copy-start.5
  18.3 1.4 collective-permute-start.3
  19.7 0.0 copy-done.4
  19.7 0.3 convert_element_type.103
  20.0 0.0 copy-done.5
  20.0 0.3 convert_element_type.102
  20.3 1.6 slice_bitcast_fusion.2
  21.9 0.0 copy-start.9
  21.9 2.2 slice_bitcast_fusion.3
  24.8 0.0 copy-start.1
  24.8 0.0 copy-done.9
  24.8 0.6 fusion.172
  25.4 0.0 collective-permute-done.2
  25.4 0.2 convert_element_type.104
  25.6 0.4 slice_bitcast_fusion.7
  26.0 0.0 collective-permute-done.3
  26.0 1.1 convert_element_type.105
  27.1 0.4 slice_bitcast_fusion.6
  27.6 0.0 copy-start.6
  27.6 0.0 copy-start.7
  27.6 0.0 copy-done.1
  27.6 0.0 copy-start
  27.6 6.6 %slice_maximum_fusion = (f32[9,65535]{1,0:T(8,128)}, f32[9,65535]{1,0:T(8,128)}) fusion(f32[1,65536]{1,0:T(1,128)S(1)} %get-tuple-element.46, f32[8,65536]{1,0:T(8,128)} %get-tuple-element.36, f32[1,65536]{1,0:T(1,128)S(1)} %get-tuple-element.45, f32[8,65536]{1,0:T(8,128)S(1)} %copy-done.1), kind=kLoop, calls=%fused_computation | loop fusion | flops 1179630 | bytes 9437112 | tf_op jit(solution)/shard_map/while/body/eval_jaxpr/concatenate | solution.py:101
  34.2 0.0 copy-done.6
  34.2 0.0 copy-done.7
  34.2 0.0 copy-done
  34.2 4.9 %slice_maximum_fusion.1 = (f32[9,65535]{1,0:T(8,128)}, f32[9,65535]{1,0:T(8,128)}) fusion(f32[1,65536]{1,0:T(1,128)S(1)} %get-tuple-element.44, f32[8,65536]{1,0:T(8,128)S(1)} %copy-done, f32[1,65536]{1,0:T(1,128)S(1)} %get-tuple-element.43, f32[8,65536]{1,0:T(8,128)S(1)} %get-tuple-element.38), kind=kLoop, calls=%fused_computation.1 | loop fusion | flops 1179630 | bytes 9437112 | tf_op jit(solution)/shard_map/while/body/eval_jaxpr/concatenate | solution.py:101
  39.1 0.0 copy-start.2
  39.1 0.0 collective-permute-done
  39.1 1.9 constant_dynamic-update-slice_fusion.1
  41.0 0.3 copy-done.2
  41.3 0.3 constant_dynamic-update-slice_fusion
  41.6 0.0 collective-permute-done.1
  41.6 1.7 constant_dynamic-update-slice_fusion.2
  43.3 6.9 %fusion.4 = f32[8,65536]{1,0:T(8,128)} fusion(f32[8,65536]{1,0:T(8,128)} %collective-permute-done.1, f32[16,65536]{1,0:T(8,128)S(1)} %constant_dynamic-update-slice_fusion.2, f32[16,65536]{1,0:T(8,128)S(1)} %get-tuple-element.41, f32[8,65536]{1,0:T(8,128)} %collective-permute-done, f32[8,65536]{1,0:T(8,128)} %param.6), kind=kLoop, calls=%fused_computation.67 | loop fusion | flops 16252928 | bytes 37748736 | tf_op jit(solution)/shard_map/add | solution.py:54
  50.2 46.0 %fusion.2 = (f32[8,65536]{1,0:T(8,128)}, f32[8,65536]{1,0:T(8,128)}, pred[8,65536]{1,0:T(8,128)(4,1)}) fusion(f32[8,65536]{1,0:T(8,128)} %get-tuple-element.40, f32[8,65536]{1,0:T(8,128)} %get-tuple-element.36, f32[8,65536]{1,0:T(8,128)S(1)} %get-tuple-element.38, f32[8,65536]{1,0:T(8,128)} %get-tuple-element.26, f32[1,65536]{1,0:T(1,128)} %copy-done.7, ...), kind=kLoop, calls=%fused_computation.56 | loop fusion | flops 100663296 | bytes 28049300 | tf_op jit(solution)/shard_map/while/body/eval_jaxpr/sub | solution.py:121
  96.2 0.0 copy-start.3
  96.2 0.0 copy-start.8
  96.2 0.0 reduce-scatter.2.cloned.1.call-update
  96.2 0.0 all-gather.3.cloned.1.call-start
  96.3 1.5 broadcast_multiply_fusion.1
  97.8 69.1 %reduce-scatter.2.cloned.1.call-done = f32[8,32768]{1,0:T(8,128)} async-done(((f32[8,65536]{1,0:T(8,128)}), f32[8,32768]{1,0:T(8,128)}) %reduce-scatter.2.cloned.1.call-update) | async-done | bytes 1048592 | tf_op jit(solution)/shard_map/reduce_scatter | solution.py:153
  166.9 0.0 copy-done.3
  166.9 0.0 copy-done.8
  166.9 1.9 fusion.104
  168.7 1.3 collective-permute-start.5
  170.0 3.1 %collective-permute-start.4 = (f32[8,32768]{1,0:T(8,128)S(1)}, f32[8,32768]{1,0:T(8,128)S(1)}, u32[]{:S(2)}, u32[]{:S(2)}) collective-permute-start(f32[8,32768]{1,0:T(8,128)S(1)} %fusion.104), channel_id=1, source_target_pairs={{0,2},{2,4},{4,6},{6,8},{8,10},{10,12},{12,14},{14,16},{16,18},{18... | collective-permute-start | bytes 3145736 | tf_op jit(solution)/shard_map/ppermute | solution.py:32
  173.1 0.1 collective-permute-done.5
  173.3 2.1 collective-permute-done.4
  175.3 4.2 %fusion.66 = f32[8,32768]{1,0:T(8,128)} fusion(f32[8,32768]{1,0:T(8,128)S(1)} %collective-permute-done.5, f32[8,32768]{1,0:T(8,128)S(1)} %fusion.104, f32[8,32768]{1,0:T(8,128)S(1)} %collective-permute-done.4), kind=kLoop, calls=%fused_computation.159 | loop fusion | flops 11796480 | bytes 4194304 | tf_op jit(solution)/shard_map/add | solution.py:54
  179.6 0.0 all-gather.3.cloned.1.call-update
  179.6 53.8 %all-gather.3.cloned.1.call-done = f32[16,32768]{1,0:T(8,128)} async-done(((f32[8,32768]{1,0:T(8,128)}), f32[16,32768]{1,0:T(8,128)}) %all-gather.3.cloned.1.call-update) | async-done | bytes 2097168 | tf_op jit(solution)/shard_map/all_gather | solution.py:159
  233.4 24.1 %multiply_reduce_fusion = (f32[]{:T(128)}, f32[8,65536]{1,0:T(8,128)S(1)}) fusion(f32[8,65536]{1,0:T(8,128)} %bitcast.23), kind=kLoop, calls=%fused_computation.95 | loop fusion | flops 17301504 | bytes 4194308 | tf_op jit(solution)/shard_map/reduce_sum | solution.py:162
  257.5 33.6 %psum.7 = f32[]{:T(128)} all-reduce(f32[]{:T(128)} %get-tuple-element.21), channel_id=1, replica_groups=mesh['rows'=16,'freq'=2] {'rows'}, use_global_device_ids=true, to_apply=%region_3.4 | all-reduce | flops 1 | bytes 8 | tf_op jit(solution)/shard_map/psum | solution.py:162
  291.8 1.5 broadcast_multiply_fusion
  (2 shorter events, 0.0 us)
Async XLA Ops:
  6.5 13.2 %copy-start.4 = (bf16[2,1,8,65536]{3,2,1,0:T(8,128)(2,1)S(1)}, bf16[2,1,8,65536]{3,2,1,0:T(8,128)(2,1)}, u32[]{:S(2)}) copy-start(bf16[2,1,8,65536]{3,2,1,0:T(8,128)(2,1)} %param.8) | copy-start | bytes 6291460
  6.5 160.3 %reduce-scatter.2.cloned.1.call-start = ((), (), s32[]{:S(2)}) async-start(), calls=%async_computation.1 | async-start | bytes 3145728 | tf_op jit(solution)/shard_map/reduce_scatter | solution.py:153
  6.5 32.5 %collective-permute-start = (f32[8,65536]{1,0:T(8,128)}, f32[8,65536]{1,0:T(8,128)}, u32[]{:S(2)}, u32[]{:S(2)}) collective-permute-start(f32[8,65536]{1,0:T(8,128)} %param.6), channel_id=1, source_target_pairs={{0,2},{2,4},{4,6},{6,8},{8,10},{10,12},{12,14},{14,16},{16,18},{18... | collective-permute-start | bytes 6291464 | tf_op jit(solution)/shard_map/ppermute | solution.py:32
  10.4 31.2 %collective-permute-start.1 = (f32[8,65536]{1,0:T(8,128)}, f32[8,65536]{1,0:T(8,128)}, u32[]{:S(2)}, u32[]{:S(2)}) collective-permute-start(f32[8,65536]{1,0:T(8,128)} %param.6), channel_id=1, source_target_pairs={{2,0},{4,2},{6,4},{8,6},{10,8},{12,10},{14,12},{16,14},{18,16},{20... | collective-permute-start | bytes 6291464 | tf_op jit(solution)/shard_map/ppermute | solution.py:35
  14.0 11.4 %collective-permute-start.2 = (bf16[2,1,1,65536]{3,0,2,1:T(2,128)(2,1)S(1)}, bf16[2,1,1,65536]{3,0,2,1:T(2,128)(2,1)S(1)}, u32[]{:S(2)}, u32[]{:S(2)}) collective-permute-start(bf16[2,1,1,65536]{3,0,2,1:T(2,128)(2,1)S(1)} %copy.9), channel_id=1, source_target_pairs={{2,0},{4,2},{6,4},{8,6},{10,8},{12,10},{14,12},{16,14},{18,16},{20... | collective-permute-start | bytes 786440 | tf_op jit(solution)/shard_map/ppermute | solution.py:43
  18.3 1.7 copy-start.5
  18.3 7.7 %collective-permute-start.3 = (bf16[2,1,1,65536]{3,0,2,1:T(2,128)(2,1)}, bf16[2,1,1,65536]{3,0,2,1:T(2,128)(2,1)}, u32[]{:S(2)}, u32[]{:S(2)}) collective-permute-start(bf16[2,1,1,65536]{3,0,2,1:T(2,128)(2,1)} %copy.10), channel_id=1, source_target_pairs={{2,0},{4,2},{6,4},{8,6},{10,8},{12,10},{14,12},{16,14},{18,16},{20... | collective-permute-start | bytes 786440 | tf_op jit(solution)/shard_map/ppermute | solution.py:43
  21.9 2.9 copy-start.9
  24.8 2.8 copy-start.1
  27.6 6.7 %copy-start.6 = (f32[1,65536]{1,0:T(1,128)}, f32[1,65536]{1,0:T(1,128)S(1)}, u32[]{:S(2)}) copy-start(f32[1,65536]{1,0:T(1,128)S(1)} %get-tuple-element.45) | copy-start | bytes 786436
  27.6 6.7 %copy-start.7 = (f32[1,65536]{1,0:T(1,128)}, f32[1,65536]{1,0:T(1,128)S(1)}, u32[]{:S(2)}) copy-start(f32[1,65536]{1,0:T(1,128)S(1)} %get-tuple-element.46) | copy-start | bytes 786436
  27.6 6.6 %copy-start = (f32[8,65536]{1,0:T(8,128)S(1)}, f32[8,65536]{1,0:T(8,128)}, u32[]{:S(2)}) copy-start(f32[8,65536]{1,0:T(8,128)} %get-tuple-element.40) | copy-start | bytes 6291460
  39.1 2.2 copy-start.2
  96.2 70.7 %copy-start.3 = (f32[8,65536]{1,0:T(8,128)S(1)}, f32[8,65536]{1,0:T(8,128)}, u32[]{:S(2)}) copy-start(f32[8,65536]{1,0:T(8,128)} %get-tuple-element.24) | copy-start | bytes 6291460
  96.2 70.7 %copy-start.8 = (pred[8,65536]{1,0:T(8,128)(4,1)S(1)}, pred[8,65536]{1,0:T(8,128)(4,1)}, u32[]{:S(2)}) copy-start(pred[8,65536]{1,0:T(8,128)(4,1)} %get-tuple-element.25) | copy-start | bytes 1572868
  96.2 137.2 %all-gather.3.cloned.1.call-start = ((), (), s32[]{:S(2)}) async-start(), calls=%async_computation.2 | async-start | bytes 3145728 | tf_op jit(solution)/shard_map/all_gather | solution.py:159
  168.7 4.6 %collective-permute-start.5 = (f32[8,32768]{1,0:T(8,128)S(1)}, f32[8,32768]{1,0:T(8,128)S(1)}, u32[]{:S(2)}, u32[]{:S(2)}) collective-permute-start(f32[8,32768]{1,0:T(8,128)S(1)} %fusion.104), channel_id=1, source_target_pairs={{2,0},{4,2},{6,4},{8,6},{10,8},{12,10},{14,12},{16,14},{18,16},{20... | collective-permute-start | bytes 3145736 | tf_op jit(solution)/shard_map/ppermute | solution.py:35
  170.0 5.3 %collective-permute-start.4 = (f32[8,32768]{1,0:T(8,128)S(1)}, f32[8,32768]{1,0:T(8,128)S(1)}, u32[]{:S(2)}, u32[]{:S(2)}) collective-permute-start(f32[8,32768]{1,0:T(8,128)S(1)} %fusion.104), channel_id=1, source_target_pairs={{0,2},{2,4},{4,6},{6,8},{8,10},{10,12},{12,14},{14,16},{16,18},{18... | collective-permute-start | bytes 3145736 | tf_op jit(solution)/shard_map/ppermute | solution.py:32
Sparse Core Ops, SparseCore 0:
  96.3 70.4 reduce-scatter.1
  179.7 53.6 all-gather.2
